TPU v7x, 32 devices: a whole 2x2x4 slice. The times are simulated.
32 devices in a mesh: groups: 2 (over x), frames: 16 (over z, y, core).
Axes of the slice: x: 2, y: 2, z: 4, core: 2. Of those that a mesh axis runs over, the one named last changes fastest.
Arguments:
- latents: bfloat16 [256, 32, 512], P(('groups', 'frames')), parts along dimension 0, may hold values from -6 to 6
- timestep: int32 [256], P(('groups', 'frames')), parts along dimension 0, may hold values from 0 to 49, as said below
- lookback: int32 [256], P(('groups', 'frames')), parts along dimension 0, may hold values from 1 to 8, as said below
- modulation: bfloat16 [2, 50, 4, 512], replicated, may hold values from -2.390625 to 2.390625
- input_weight: bfloat16 [2, 512, 2304], replicated, may hold values from -0.25 to 0.25
- step_weight: bfloat16 [2, 512, 16], replicated, may hold values from -0.25 to 0.25
- conv_weight: float32 [2, 4, 1280], replicated, may hold values from -3 to 3
- step_bias: float32 [2, 50, 16], replicated, may hold values from -3 to 2
- decay_log: float32 [2, 16], replicated
- skip_gain: float32 [2, 16], replicated, may hold values from -2 to 2
- norm_gain: float32 [2, 1024], replicated, may hold values from 0.1 to 1.9
- output_weight: bfloat16 [2, 1024, 512], replicated, may hold values from -0.1875 to 0.1875
- query_weight: bfloat16 [2, 512, 512], replicated
- memory_weight: bfloat16 [2, 512, 1024], replicated
- merge_weight: bfloat16 [2, 512, 512], replicated, may hold values from -0.25 to 0.25
Outputs:
- denoised: float32 [256, 32, 512], P(('groups', 'frames')), parts along dimension 0
There are 2 independent parts, one for each index of `groups`. A program takes and returns all parts, laid end to end along the dimension named above; an argument that names none is the same for every part. Nothing has to cross between parts.
Inputs may be any that keep to these rules, and one draw needn't show every extreme that they name: timestep is the same for all frames of each aligned run of 8 frames. lookback[f] counts the preceding frames that frame f attends to; 8 occurs in every draw.
All inputs are finite; a program needn't handle non-finite values.
Results may differ from a plain program's by a relative error of at most 0.01.
Values may be sent and summed in bfloat16 or wider, within the bound.
A program may use at most 128 MiB of HBM per device.

v0:
```python
import jax
import jax.numpy as jnp
from jax import lax
from jax.sharding import PartitionSpec as P

HEADS = 16
HEAD_DIM = 64
STATE = 128
ATT_HEADS = 8
NSTEPS = 50
LAYERS = 2
CONV = 4
SPAN = 128
WINDOW = 8


EPS = 1e-06
HEAD_EPS = 1e-05


def from_behind(value, axis, steps):
    count = lax.axis_size(axis)
    initial, last = (max(0, -steps), min(count, count - steps))
    return lax.ppermute(value, axis, [(source, source + steps) for source in range(initial, last)])


def carried_in(value, axis, combine, identity):
    devices, place = (lax.axis_size(axis), lax.axis_index(axis))
    everything = jax.tree.map(
        lambda part, kind: lax.all_gather(part.astype(kind), axis),
        value,
        (jnp.bfloat16, jnp.bfloat16),
    )
    start = jax.tree.map(
        lambda part, zero: jnp.broadcast_to(jnp.asarray(zero, part.dtype), part.shape),
        value,
        identity,
    )

    def hop(k, before):
        reached = k < place
        new = combine(
            before, jax.tree.map(lambda part, own: part[k].astype(own.dtype), everything, value)
        )
        return jax.tree.map(lambda a, b: jnp.where(reached, a, b), new, before)

    return lax.fori_loop(0, devices, hop, start)


def rms_rows(values):
    return values * lax.rsqrt(jnp.mean(values * values, axis=-1, keepdims=True) + EPS)


def modulated(resid, shift, scale):
    normed = rms_rows(resid)
    return (normed * (1.0 + scale[:, None, :]) + shift[:, None, :]).astype(jnp.bfloat16)


def conv_silu(extended, weights, count):
    total = weights[0][None, :] * extended[0:count].astype(jnp.float32)
    for offset in range(1, CONV):
        total = total + weights[offset][None, :] * extended[offset : offset + count].astype(
            jnp.float32
        )
    return jax.nn.silu(total).astype(jnp.bfloat16)


def span_terms(values, input_map, output_map, log_decay, step_size):
    count = values.shape[0] // SPAN
    by_head = values.reshape(count, SPAN, HEADS, HEAD_DIM)
    in_blocks = input_map.reshape(count, SPAN, STATE)
    out_blocks = output_map.reshape(count, SPAN, STATE)
    cumulated = jnp.cumsum(log_decay.reshape(count, SPAN, HEADS), axis=1).transpose(0, 2, 1)
    steps = step_size.reshape(count, SPAN, HEADS).transpose(0, 2, 1)
    affinity = jnp.einsum("cqn,csn->cqs", out_blocks, in_blocks, preferred_element_type=jnp.float32)
    position = jnp.arange(SPAN)
    lower = position[:, None] >= position[None, :]
    gaps = cumulated[:, :, :, None] - cumulated[:, :, None, :]
    gaps = jnp.where(lower[None, None], gaps, -jnp.inf)
    mixing = (affinity[:, None] * jnp.exp(gaps) * steps[:, :, None, :]).astype(jnp.bfloat16)
    y_local = jnp.einsum("chqs,cshp->cqhp", mixing, by_head, preferred_element_type=jnp.float32)
    edge = jnp.exp(cumulated[:, :, -1:] - cumulated) * steps
    weighted = (in_blocks[:, None, :, :].astype(jnp.float32) * edge[:, :, :, None]).astype(
        jnp.bfloat16
    )
    states = jnp.einsum("cshp,chsn->chpn", by_head, weighted, preferred_element_type=jnp.float32)
    return (y_local, states, cumulated, out_blocks)


def finish_mixer(resid, y_total, values, gate_half, skip, gain, weight):
    rows = values.shape[0]
    mixed = y_total.reshape(rows, HEADS * HEAD_DIM) + jnp.repeat(skip, HEAD_DIM)[
        None, :
    ] * values.astype(jnp.float32)
    gated = (mixed * jax.nn.silu(gate_half.astype(jnp.float32))).reshape(rows, HEADS, HEAD_DIM)
    gated = gated * lax.rsqrt(jnp.mean(gated * gated, axis=-1, keepdims=True) + HEAD_EPS)
    normed = (gated.reshape(rows, HEADS * HEAD_DIM) * gain[None, :]).astype(jnp.bfloat16)
    update = jnp.dot(normed, weight, preferred_element_type=jnp.float32)
    return resid + update.reshape(resid.shape)


def combine_states(earlier, later):
    return (earlier[0] * later[0], later[0][:, None, None] * earlier[1] + later[1])


def attend(query_block, key_block, query_frame, key_frame, reach):
    count, tok_frame, attn = query_block.shape
    heads = attn // HEAD_DIM
    queries = query_block.reshape(count * tok_frame, heads, HEAD_DIM)
    key_rows = key_block[:, :, :attn].reshape(-1, heads, HEAD_DIM)
    value_rows = key_block[:, :, attn:].reshape(-1, heads, HEAD_DIM)
    scores = jnp.einsum(
        "qhd,khd->hqk", queries, key_rows, preferred_element_type=jnp.float32
    ) * HEAD_DIM ** (-0.5)
    allowed = (
        (key_frame[None, :] >= 0)
        & (key_frame[None, :] <= query_frame[:, None])
        & (key_frame[None, :] >= query_frame[:, None] - reach[:, None])
    )
    allowed = jnp.repeat(jnp.repeat(allowed, tok_frame, axis=0), tok_frame, axis=1)
    scores = jnp.where(allowed[None], scores, -1e30)
    top = jnp.max(scores, axis=-1, keepdims=True)
    weights = jnp.exp(scores - top)
    probs = (weights / jnp.sum(weights, axis=-1, keepdims=True)).astype(jnp.bfloat16)
    mixed = jnp.einsum("hqk,khd->qhd", probs, value_rows, preferred_element_type=jnp.float32)
    return mixed.astype(jnp.bfloat16).reshape(count, tok_frame, attn)


def shards(
    latents,
    timestep,
    lookback,
    modulation,
    input_weight,
    step_weight,
    conv_weight,
    step_bias,
    decay_log,
    skip_gain,
    norm_gain,
    output_weight,
    query_weight,
    memory_weight,
    merge_weight,
):
    frames_dev, tok_frame, width = latents.shape
    inner = HEADS * HEAD_DIM
    attn = ATT_HEADS * HEAD_DIM
    base = lax.axis_index("frames") * frames_dev
    onehot = (timestep[:, None] == jnp.arange(NSTEPS, dtype=jnp.int32)[None, :]).astype(
        jnp.bfloat16
    )
    onehot_wide = onehot.astype(jnp.float32)
    resid = latents.astype(jnp.float32)
    for layer in range(LAYERS):
        mods = jnp.dot(
            onehot, modulation[layer].reshape(NSTEPS, 4 * width), preferred_element_type=jnp.float32
        ).reshape(frames_dev, 4, width)
        frame_bias = jnp.dot(onehot_wide, step_bias[layer], precision=lax.Precision.HIGHEST)
        u_rows = modulated(resid, mods[:, 0], mods[:, 1]).reshape(-1, width)
        projected = jnp.dot(u_rows, input_weight[layer], preferred_element_type=jnp.float32).astype(
            jnp.bfloat16
        )
        gate_half = projected[:, :inner]
        mixed_in = projected[:, inner:]
        step_raw = jnp.dot(u_rows, step_weight[layer], preferred_element_type=jnp.float32)
        step_raw = (
            step_raw.reshape(frames_dev, tok_frame, HEADS) + frame_bias[:, None, :]
        ).reshape(-1, HEADS)
        rows = mixed_in.shape[0]
        tail = from_behind(mixed_in[rows - (CONV - 1) :], "frames", 1)
        extended = jnp.concatenate([tail, mixed_in], axis=0)
        act = conv_silu(extended, conv_weight[layer], rows)
        values = act[:, :inner]
        input_map = act[:, inner : inner + STATE]
        output_map = act[:, inner + STATE :]
        step_size = jax.nn.softplus(step_raw)
        log_decay = -jnp.exp(decay_log[layer])[None, :] * step_size
        y_local, states, cumulated, out_blocks = span_terms(
            values, input_map, output_map, log_decay, step_size
        )
        ends = cumulated[:, :, -1]

        def walk(carry, item):
            state, end_log = item
            return (jnp.exp(end_log)[:, None, None] * carry + state, carry)

        dev_state, before = lax.scan(
            walk, jnp.zeros((HEADS, HEAD_DIM, STATE), jnp.float32), (states, ends)
        )
        dev_decay = jnp.exp(jnp.sum(ends, axis=0))
        scanned = carried_in(
            (dev_decay, dev_state),
            "frames",
            combine_states,
            (jnp.ones_like(dev_decay), jnp.zeros_like(dev_state)),
        )
        incoming = scanned[1]
        prefix = jnp.exp(jnp.cumsum(ends, axis=0) - ends)
        entering = before + prefix[:, :, None, None] * incoming[None]
        y_carry = jnp.einsum(
            "cqn,chpn->cqhp",
            out_blocks.astype(jnp.float32),
            entering,
            precision=lax.Precision.HIGHEST,
        )
        y_carry = y_carry * jnp.exp(cumulated).transpose(0, 2, 1)[:, :, :, None]
        hidden = finish_mixer(
            resid,
            y_local + y_carry,
            values,
            gate_half,
            skip_gain[layer],
            norm_gain[layer],
            output_weight[layer],
        )
        a_rows = modulated(hidden, mods[:, 2], mods[:, 3]).reshape(-1, width)
        queries = (
            jnp.dot(a_rows, query_weight[layer], preferred_element_type=jnp.float32)
            .astype(jnp.bfloat16)
            .reshape(frames_dev, tok_frame, attn)
        )
        memory = (
            jnp.dot(a_rows, memory_weight[layer], preferred_element_type=jnp.float32)
            .astype(jnp.bfloat16)
            .reshape(frames_dev, tok_frame, 2 * attn)
        )
        memory_tail = from_behind(memory, "frames", 1)
        keyed = jnp.concatenate([memory_tail, memory], axis=0)
        query_frame = base + 0 + jnp.arange(WINDOW, dtype=jnp.int32)
        key_frame = base + 0 - WINDOW + jnp.arange(2 * WINDOW, dtype=jnp.int32)
        outputs = attend(queries, keyed, query_frame, key_frame, lookback)
        attended = outputs.reshape(-1, attn)
        update = jnp.dot(attended, merge_weight[layer], preferred_element_type=jnp.float32)
        resid = hidden + update.reshape(hidden.shape)
    return resid


def solution(mesh):
    return jax.shard_map(
        shards,
        mesh=mesh,
        in_specs=(
            P(("groups", "frames"), None, None),
            P(("groups", "frames")),
            P(("groups", "frames")),
            P(),
            P(),
            P(),
            P(),
            P(),
            P(),
            P(),
            P(),
            P(),
            P(),
            P(),
            P(),
        ),
        out_specs=P(("groups", "frames"), None, None),
        check_vma=False,
    )
```

profile of v0, /device:TPU:8, one launch (start us, length us, event | category | flops | bytes accessed | tf_op | source)
XLA Modules:
  0.0 264.7 jit_solution(11436102423662947714)
XLA Ops:
  6.5 1.9 slice_bitcast_fusion
  9.9 2.5 convolution_convert_fusion.1
  12.4 1.9 collective-permute-start
  23.0 1.7 while.54
  25.7 1.3 dynamic-slice
  28.4 26.1 %all-reduce = bf16[256]{0:T(256)(128)(2,1)S(1)} all-reduce(bf16[256]{0:T(256)(128)(2,1)S(1)} %dynamic-update-slice), channel_id=2, replica_groups=mesh['groups'=2,'frames'=16] {'frames'}, use_global_device_ids=true, to_apply=%add | all-reduce | flops 256 | bytes 1024
  55.3 1.3 slice_bitcast_fusion.6
  60.4 1.9 convolution_bitcast_fusion.1
  62.4 15.5 %all-gather.7.cloned.1.call-done = bf16[256,64,128]{2,1,0:T(8,128)(2,1)} async-done(((bf16[16,64,128]{2,1,0:T(8,128)(2,1)}), bf16[256,64,128]{2,1,0:T(8,128)(2,1)}) %all-gather.7.cloned.1.call-update) | async-done | bytes 4194320 | tf_op jit(solution)/shard_map/all_gather | solution.py:30
  77.9 18.1 %while.55 = (s32[]{:T(128)}, f32[16,64,128]{2,1,0:T(8,128)S(1)}, s32[]{:T(128)}, bf16[16,16]{1,0:T(8,128)(2,1)S(1)}, bf16[16,16,64,128]{3,2,1,0:T(8,128)(2,1)}, /*index=5*/s32[]{:T(128)}, s32[]{:T(128)}) while((s32[]{:T(128)}, f32[16,64,128]{2,1,0:T(8,128)S(1)}, s32[]{:T(128)}, bf16[16,16]{1,0:T(8,128)(2,1)S(1)}, ...), condition=%wide.region_7.8_spmd.clone, body=%wide.region_6.7_spmd.clone.sunk | while | flops 655380 | bytes 1310985 | solution.py:47
  79.0 1.1 fusion.166
  80.2 1.1 fusion.166
  81.3 1.1 fusion.166
  82.4 1.1 fusion.166
  83.6 1.1 fusion.166
  84.7 1.1 fusion.166
  85.8 1.1 fusion.166
  87.0 1.1 fusion.166
  88.1 1.1 fusion.166
  89.2 1.1 fusion.166
  90.4 1.1 fusion.166
  91.5 1.1 fusion.166
  92.6 1.1 fusion.166
  93.8 1.1 fusion.166
  96.0 2.0 fusion.23
  98.0 2.1 copy.224
  100.0 2.0 reshape.376
  102.0 2.4 fusion.129
  104.5 1.6 copy.193
  107.2 1.6 copy.194
  108.8 1.6 multiply_convert_fusion.11
  112.6 2.3 collective-permute-start.1
  116.8 1.3 convolution_convert_fusion.5
  118.3 5.7 %collective-permute-done.1 = bf16[8,32,1024]{2,1,0:T(8,128)(2,1)S(1)} collective-permute-done((bf16[8,32,1024]{2,1,0:T(8,128)(2,1)S(1)}, bf16[8,32,1024]{2,1,0:T(8,128)(2,1)S(1)}, u32[]{:S(2)}, u32[]{:S(2)}) %collective-permute-start.1) | collective-permute-done | bytes 524320 | tf_op jit(solution)/shard_map/ppermute | solution.py:24
  124.6 1.5 reshape.332
  127.1 2.1 fusion.133
  133.6 2.5 convolution_convert_fusion
  136.1 1.9 collective-permute-start.2
  138.8 3.2 %collective-permute-done.2 = bf16[3,1280]{1,0:T(4,128)(2,1)S(1)} collective-permute-done((bf16[3,1280]{1,0:T(4,128)(2,1)S(1)}, bf16[3,1280]{1,0:T(4,128)(2,1)S(1)}, u32[]{:S(2)}, u32[]{:S(2)}) %collective-permute-start.2) | collective-permute-done | bytes 7712 | tf_op jit(solution)/shard_map/ppermute | solution.py:24
  144.5 1.8 fusion.37
  146.3 1.1 broadcast.160
  147.4 3.3 %while.56 = (s32[]{:T(128)}, f32[16,64,128]{2,1,0:T(8,128)S(1)}, f32[2,16,64,128]{3,2,1,0:T(8,128)}, f32[2,16]{1,0:T(2,128)}, f32[2,16,64,128]{3,2,1,0:T(8,128)S(1)}, /*index=5*/s32[]{:T(128)}, s32[]{:T(128)}) while((s32[]{:T(128)}, f32[16,64,128]{2,1,0:T(8,128)S(1)}, f32[2,16,64,128]{3,2,1,0:T(8,128)}, f32[2,16]{1,0:T(2,128)}, ...), condition=%wide.region_15.16_spmd.clone, body=%wide.region_14.15_spmd.clone.sunk | while | flops 524291 | bytes 2622240 | solution.py:188
  154.5 23.4 %all-reduce.1 = bf16[256]{0:T(256)(128)(2,1)S(1)} all-reduce(bf16[256]{0:T(256)(128)(2,1)S(1)} %dynamic-update-slice.1), channel_id=4, replica_groups=mesh['groups'=2,'frames'=16] {'frames'}, use_global_device_ids=true, to_apply=%add.1 | all-reduce | flops 256 | bytes 1024
  178.7 1.3 subtract_exponential_fusion.2
  180.1 2.6 %convolution_bitcast_fusion = f32[2,128,16,64]{1,3,2,0:T(8,128)} fusion(bf16[2,128,16,64]{1,3,2,0:T(8,128)(2,1)S(1)} %copy.211, f32[2,16,128]{2,1,0:T(8,128)} %get-tuple-element.398, f32[2,16,128]{2,1,0:T(8,128)S(1)} %bitcast.266, f32[2,128,128]{2,1,0:T(8,128)S(1)} %fusion.136, pred[128,128]{1,0:T(8,128)(4,1)} %copy-done.32), kind=kOutput, calls=%fused_computation.48 | convolution fusion | flops 69730304 | bytes 1753088 | tf_op jit(solution)/shard_map/chqs,cshp->cqhp/dot_general | solution.py:81
  182.7 17.9 %all-gather.9.cloned.1.call-done = bf16[256,64,128]{2,1,0:T(8,128)(2,1)} async-done(((bf16[16,64,128]{2,1,0:T(8,128)(2,1)}), bf16[256,64,128]{2,1,0:T(8,128)(2,1)}) %all-gather.9.cloned.1.call-update) | async-done | bytes 4194320 | tf_op jit(solution)/shard_map/all_gather | solution.py:30
  200.6 18.1 %while.57 = (s32[]{:T(128)}, f32[16,64,128]{2,1,0:T(8,128)S(1)}, s32[]{:T(128)}, bf16[16,16]{1,0:T(8,128)(2,1)S(1)}, bf16[16,16,64,128]{3,2,1,0:T(8,128)(2,1)}, /*index=5*/s32[]{:T(128)}, s32[]{:T(128)}) while((s32[]{:T(128)}, f32[16,64,128]{2,1,0:T(8,128)S(1)}, s32[]{:T(128)}, bf16[16,16]{1,0:T(8,128)(2,1)S(1)}, ...), condition=%wide.region_19.20_spmd.clone, body=%wide.region_18.19_spmd.clone.sunk | while | flops 655380 | bytes 1310985 | solution.py:47
  200.7 1.1 fusion.168
  201.8 1.1 fusion.168
  202.9 1.1 fusion.168
  204.1 1.1 fusion.168
  205.2 1.1 fusion.168
  218.8 2.3 fusion.22
  221.1 2.1 copy.225
  223.1 2.0 reshape.377
  225.2 2.4 fusion.128
  227.6 1.6 copy.216
  230.3 1.6 copy.217
  231.9 1.6 multiply_convert_fusion.10
  235.7 2.2 collective-permute-start.3
  238.3 8.8 %collective-permute-done.3 = bf16[8,32,1024]{2,1,0:T(8,128)(2,1)S(1)} collective-permute-done((bf16[8,32,1024]{2,1,0:T(8,128)(2,1)S(1)}, bf16[8,32,1024]{2,1,0:T(8,128)(2,1)S(1)}, u32[]{:S(2)}, u32[]{:S(2)}) %collective-permute-start.3) | collective-permute-done | bytes 524320 | tf_op jit(solution)/shard_map/ppermute | solution.py:24
  248.7 3.7 %fusion.134 = (f32[8,256]{1,0:T(8,128)S(1)}, f32[8,256,512]{2,1,0:T(8,128)}) fusion(f32[8,256,512]{2,1,0:T(8,128)S(1)} %fusion.43, pred[256,512]{1,0:T(8,128)(4,1)S(1)} %copy-done.12), kind=kOutput, calls=%fused_computation.246 | output fusion | flops 6291967 | bytes 8527872 | tf_op jit(solution)/shard_map/sub | solution.py:123
  252.9 3.2 %fusion.27 = bf16[256,8,64]{0,2,1:T(8,128)(2,1)S(1)} fusion(f32[8,256,512]{2,1,0:T(8,128)} %get-tuple-element.416, f32[8,256]{1,0:T(8,128)S(1)} %get-tuple-element.415, bf16[512,8,64]{2,1,0:T(8,128)(2,1)S(1)} %reshape.343), kind=kOutput, calls=%fused_computation.67 | convolution fusion | flops 136445952 | bytes 4988928 | tf_op jit(solution)/shard_map/hqk,khd->qhd/dot_general | solution.py:125
  256.8 1.1 convolution_add_fusion.2
  (279 shorter events, 61.0 us)
Async XLA Ops:
  6.5 2.1 copy-start.36
  6.5 3.0 %copy-start.7 = (bf16[8,32,512]{2,1,0:T(8,128)(2,1)S(1)}, bf16[8,32,512]{2,1,0:T(8,128)(2,1)}, u32[]{:S(2)}) copy-start(bf16[8,32,512]{2,1,0:T(8,128)(2,1)} %param.23) | copy-start | bytes 786436
  6.5 71.3 %all-gather.7.cloned.1.call-start = ((), (), s32[]{:S(2)}) async-start(), calls=%async_computation | async-start | bytes 4456448 | tf_op jit(solution)/shard_map/all_gather | solution.py:30
  9.8 4.5 %copy-start.45 = (f32[2,50,16]{1,2,0:T(8,128)S(1)}, f32[2,50,16]{1,2,0:T(8,128)}, u32[]{:S(2)}) copy-start(f32[2,50,16]{1,2,0:T(8,128)} %param.30) | copy-start | bytes 19204
  9.8 4.7 %copy-start.25 = (bf16[2,512,16]{1,2,0:T(8,128)(2,1)S(1)}, bf16[2,512,16]{1,2,0:T(8,128)(2,1)}, u32[]{:S(2)}) copy-start(bf16[2,512,16]{1,2,0:T(8,128)(2,1)} %param.28) | copy-start | bytes 98308
  9.8 5.1 %copy-start.39 = (f32[2,16]{1,0:T(2,128)S(1)}, f32[2,16]{1,0:T(2,128)}, u32[]{:S(2)}) copy-start(f32[2,16]{1,0:T(2,128)} %param.31) | copy-start | bytes 388
  9.9 7.9 %copy-start.19 = (f32[2,4,1280]{2,1,0:T(4,128)S(1)}, f32[2,4,1280]{2,1,0:T(4,128)}, u32[]{:S(2)}) copy-start(f32[2,4,1280]{2,1,0:T(4,128)} %param.29) | copy-start | bytes 122884
  12.3 6.1 %copy-start = (bf16[256,2304]{1,0:T(8,128)(2,1)}, bf16[256,2304]{1,0:T(8,128)(2,1)S(1)}, u32[]{:S(2)}) copy-start(bf16[256,2304]{1,0:T(8,128)(2,1)S(1)} %convolution_convert_fusion.1) | copy-start | bytes 3538948
  12.4 6.2 %collective-permute-start = (bf16[3,1280]{1,0:T(4,128)(2,1)S(1)}, bf16[3,1280]{1,0:T(4,128)(2,1)S(1)}, u32[]{:S(2)}, u32[]{:S(2)}) collective-permute-start(bf16[3,1280]{1,0:T(4,128)(2,1)S(1)} %slice.272), channel_id=1, source_target_pairs={{0,1},{1,2},{2,3},{3,4},{4,5},{5,6},{6,7},{7,8},{8,9},{9,10},{10,1... | collective-permute-start | bytes 23048 | tf_op jit(solution)/shard_map/ppermute | solution.py:24
  17.1 0.6 copy-start.29
  21.0 0.8 copy-start.2
  24.7 33.9 %copy-start.40 = (s32[8]{0:T(128)S(1)}, s32[8]{0:T(128)}, u32[]{:S(2)}) copy-start(s32[8]{0:T(128)} %param.25) | copy-start | bytes 100
  24.8 33.9 %copy-start.30 = (f32[2,16]{1,0:T(2,128)S(1)}, f32[2,16]{1,0:T(2,128)}, u32[]{:S(2)}) copy-start(f32[2,16]{1,0:T(2,128)} %get-tuple-element.639) | copy-start | bytes 388
  24.8 33.9 %copy-start.37 = (s32[8]{0:T(128)S(1)}, s32[8]{0:T(128)}, u32[]{:S(2)}) copy-start(s32[8]{0:T(128)} %param.24) | copy-start | bytes 100
  24.8 33.9 %copy-start.46 = (f32[2,50,16]{1,2,0:T(8,128)S(1)}, f32[2,50,16]{1,2,0:T(8,128)}, u32[]{:S(2)}) copy-start(f32[2,50,16]{1,2,0:T(8,128)} %param.30) | copy-start | bytes 19204
  24.8 34.7 %copy-start.33 = (f32[2,1024]{1,0:T(2,128)S(1)}, f32[2,1024]{1,0:T(2,128)}, u32[]{:S(2)}) copy-start(f32[2,1024]{1,0:T(2,128)} %param.33) | copy-start | bytes 24580
  24.8 35.6 %copy-start.3 = (bf16[2,128,16,64]{1,3,2,0:T(8,128)(2,1)S(1)}, bf16[2,128,16,64]{1,3,2,0:T(8,128)(2,1)}, u32[]{:S(2)}) copy-start(bf16[2,128,16,64]{1,3,2,0:T(8,128)(2,1)} %copy-done.2) | copy-start | bytes 1572868
  24.8 35.6 %copy-start.28 = (f32[2,16,128]{2,1,0:T(8,128)S(1)}, f32[2,16,128]{2,1,0:T(8,128)}, u32[]{:S(2)}) copy-start(f32[2,16,128]{2,1,0:T(8,128)} %get-tuple-element.400) | copy-start | bytes 49156
  25.6 175.1 %all-gather.9.cloned.1.call-start = ((), (), s32[]{:S(2)}) async-start(), calls=%async_computation.1 | async-start | bytes 4456448 | tf_op jit(solution)/shard_map/all_gather | solution.py:30
  58.6 3.8 %copy-start.32 = (pred[128,128]{1,0:T(8,128)(4,1)}, pred[128,128]{1,0:T(8,128)(4,1)S(1)}, u32[]{:S(2)}) copy-start(pred[128,128]{1,0:T(8,128)(4,1)S(1)} %iota_compare_fusion) | copy-start | bytes 49156
  108.8 1.7 copy-start.8
  108.8 1.8 copy-start.9
  110.4 0.8 copy-start.14
  110.5 0.8 copy-start.15
  110.5 1.6 copy-start.42
  111.1 3.8 %copy-start.41 = (s32[16]{0:T(128)S(1)}, s32[16]{0:T(128)}, u32[]{:S(2)}) copy-start(s32[16]{0:T(128)} %iota_add_fusion.1) | copy-start | bytes 196
  112.6 11.4 %collective-permute-start.1 = (bf16[8,32,1024]{2,1,0:T(8,128)(2,1)S(1)}, bf16[8,32,1024]{2,1,0:T(8,128)(2,1)S(1)}, u32[]{:S(2)}, u32[]{:S(2)}) collective-permute-start(bf16[8,32,1024]{2,1,0:T(8,128)(2,1)S(1)} %bitcast.253), channel_id=1, source_target_pairs={{0,1},{1,2},{2,3},{3,4},{4,5},{5,6},{6,7},{7,8},{8,9},{9,10},{10,1... | collective-permute-start | bytes 1572872 | tf_op jit(solution)/shard_map/ppermute | solution.py:24
  126.2 0.9 copy-start.11
  127.1 2.1 copy-start.6
  129.2 1.7 copy-start.4
  130.2 1.1 copy-start.18
  130.2 1.2 copy-start.26
  130.2 1.2 copy-start.34
  130.5 1.3 copy-start.38
  133.6 4.5 %copy-start.31 = (f32[2,16]{1,0:T(2,128)}, f32[2,16]{1,0:T(2,128)S(1)}, u32[]{:S(2)}) copy-start(f32[2,16]{1,0:T(2,128)S(1)} %get-tuple-element.588) | copy-start | bytes 388
  133.6 8.4 %copy-start.21 = (f32[1280]{0:T(1024)S(1)}, f32[1280]{0:T(1024)}, u32[]{:S(2)}) copy-start(f32[1280]{0:T(1024)} %get-tuple-element.327) | copy-start | bytes 15364
  133.6 8.4 %copy-start.22 = (f32[1280]{0:T(1024)S(1)}, f32[1280]{0:T(1024)}, u32[]{:S(2)}) copy-start(f32[1280]{0:T(1024)} %get-tuple-element.328) | copy-start | bytes 15364
  133.6 8.4 %copy-start.23 = (f32[1280]{0:T(1024)S(1)}, f32[1280]{0:T(1024)}, u32[]{:S(2)}) copy-start(f32[1280]{0:T(1024)} %get-tuple-element.333) | copy-start | bytes 15364
  133.6 8.4 %copy-start.24 = (f32[1280]{0:T(1024)S(1)}, f32[1280]{0:T(1024)}, u32[]{:S(2)}) copy-start(f32[1280]{0:T(1024)} %get-tuple-element.334) | copy-start | bytes 15364
  136.1 6.9 %copy-start.1 = (bf16[256,2304]{1,0:T(8,128)(2,1)}, bf16[256,2304]{1,0:T(8,128)(2,1)S(1)}, u32[]{:S(2)}) copy-start(bf16[256,2304]{1,0:T(8,128)(2,1)S(1)} %convolution_convert_fusion) | copy-start | bytes 3538948
  136.1 5.9 %collective-permute-start.2 = (bf16[3,1280]{1,0:T(4,128)(2,1)S(1)}, bf16[3,1280]{1,0:T(4,128)(2,1)S(1)}, u32[]{:S(2)}, u32[]{:S(2)}) collective-permute-start(bf16[3,1280]{1,0:T(4,128)(2,1)S(1)} %slice.289), channel_id=1, source_target_pairs={{0,1},{1,2},{2,3},{3,4},{4,5},{5,6},{6,7},{7,8},{8,9},{9,10},{10,1... | collective-permute-start | bytes 23048 | tf_op jit(solution)/shard_map/ppermute | solution.py:24
  200.6 18.1 %copy-start.13 = (f32[2,128,16]{1,2,0:T(8,128)S(1)}, f32[2,128,16]{1,2,0:T(8,128)}, u32[]{:S(2)}) copy-start(f32[2,128,16]{1,2,0:T(8,128)} %copy.213) | copy-start | bytes 49156
  200.6 18.1 %copy-start.35 = (f32[2,16]{1,0:T(2,128)S(1)}, f32[2,16]{1,0:T(2,128)}, u32[]{:S(2)}) copy-start(f32[2,16]{1,0:T(2,128)} %subtract_exponential_fusion.2) | copy-start | bytes 388
  223.1 2.0 copy-start.20
  229.2 2.8 %copy-start.27 = (f32[1,1024]{1,0:T(1,128)S(1)}, f32[1,1024]{1,0:T(1,128)}, u32[]{:S(2)}) copy-start(f32[1,1024]{1,0:T(1,128)} %get-tuple-element.401) | copy-start | bytes 12292
  231.9 1.8 copy-start.10
  233.6 0.7 copy-start.16
  233.6 0.7 copy-start.17
  233.6 1.6 copy-start.43
  234.2 3.6 %copy-start.44 = (bf16[2,512,512]{2,1,0:T(8,128)(2,1)S(1)}, bf16[2,512,512]{2,1,0:T(8,128)(2,1)}, u32[]{:S(2)}) copy-start(bf16[2,512,512]{2,1,0:T(8,128)(2,1)} %param.35) | copy-start | bytes 3145732
  235.7 11.4 %collective-permute-start.3 = (bf16[8,32,1024]{2,1,0:T(8,128)(2,1)S(1)}, bf16[8,32,1024]{2,1,0:T(8,128)(2,1)S(1)}, u32[]{:S(2)}, u32[]{:S(2)}) collective-permute-start(bf16[8,32,1024]{2,1,0:T(8,128)(2,1)S(1)} %bitcast.255), channel_id=1, source_target_pairs={{0,1},{1,2},{2,3},{3,4},{4,5},{5,6},{6,7},{7,8},{8,9},{9,10},{10,1... | collective-permute-start | bytes 1572872 | tf_op jit(solution)/shard_map/ppermute | solution.py:24
  247.7 0.9 copy-start.12
  252.9 3.9 %copy-start.5 = (bf16[2,512,512]{2,1,0:T(8,128)(2,1)S(1)}, bf16[2,512,512]{2,1,0:T(8,128)(2,1)}, u32[]{:S(2)}) copy-start(bf16[2,512,512]{2,1,0:T(8,128)(2,1)} %param.37) | copy-start | bytes 3145732
Sparse Core Ops, SparseCore 0:
  25.7 52.1 all-gather.6
  151.7 48.9 all-gather.8
where the time goes:
time: 267 us; the launch traced here: 265 us
  other arithmetic  66 us (25%)
  waiting for transfers between devices  51.1 us (19%)
  blocking collectives  49.4 us (19%)
  local copies, waits for them, and re-layouts  44 us (16%)
  matrix products  29.5 us (11%)
  between operations  15.2 us (6%)
  starting transfers between devices  8.38 us (3%)
    unnamed x2, blocking collectives  49.4 us
    select_n x32, other arithmetic, hop(): return jax.tree.map(lambda a, b: jnp.where(reached, a, b), new, before)  34.9 us
    all_gather x2, waiting for transfers between devices, carried_in(): lax.all_gather(part.astype(kind), axis)  33.4 us
    ppermute x4, waiting for transfers between devices, from_behind(): lax.ppermute(value, axis, [(source, source + steps) for source in range(i...  17.7 us
    unnamed x104, local copies, waits for them, and re-layouts  8.46 us
    ppermute x4, starting transfers between devices, from_behind(): lax.ppermute(value, axis, [(source, source + steps) for source in range(i...  8.34 us
    reshape x4, local copies, waits for them, and re-layouts, finish_mixer(): y_total.reshape(rows, HEADS * HEAD_DIM)  8.18 us
    sub x2, other arithmetic, attend(): weights = jnp.exp(scores - top)  5.78 us
  transfers between devices with their start and end apart: 6, of which 5 were waited for; matrix products, arithmetic and copies ran while one was open for 10% of the time, Pallas kernels for 0%

commit v1 on v0

v1 whole, which is shorter than its diff:
```python
import functools

import jax
import jax.numpy as jnp
from jax import lax
from jax.experimental import pallas as pl
from jax.experimental.pallas import tpu as pltpu
from jax.sharding import PartitionSpec as P

HEADS = 16
HEAD_DIM = 64
STATE = 128
ATT_HEADS = 8
LAYERS = 2
CONV = 4
SPAN = 128
WINDOW = 8
EPS = 1e-06
HEAD_EPS = 1e-05
LANES = 128
INNER = HEADS * HEAD_DIM
ATTN = ATT_HEADS * HEAD_DIM
PAIRS = INNER // LANES
F32 = jnp.float32
BF16 = jnp.bfloat16
HIGH = lax.Precision.HIGHEST
MESH = pl.DeviceIdType.MESH


def mm(a, b):
    return jnp.dot(a, b, preferred_element_type=F32)


def mm_t(a, b):
    return lax.dot_general(a, b, (((1,), (1,)), ((), ())), preferred_element_type=F32)


def sigmoid(x):
    return 0.5 * jnp.tanh(0.5 * x) + 0.5


def iota(shape, dim):
    return lax.broadcasted_iota(jnp.int32, shape, dim)


def kernel(
    n,
    x_ref, ts_ref, lb_ref, mod_ref, win_hbm, ws_ref, conv_ref, sbias_ref, dlog_ref, skip_ref,
    gain_ref, wout_hbm, wq_hbm, wm_hbm, wg_hbm,
    out_ref,
    win, wout, wq, wm, wg, wsem,
    hid, ubuf, gate, ext, act, yloc, gbuf, tri, expand, bias, ones,
    s1, r1, s2, r2, s1s, s1r, s2s, s2r,
    tsend, trecv, tss, tsr, asend, arecv, ass, asr,
    qb, kv, kvp, oacc, mstat, lstat,
):
    rows, width = x_ref.shape
    spans = rows // SPAN
    tok = rows // WINDOW
    part = r2.shape[2]
    me = lax.axis_index("frames")
    nxt = lax.rem(me + 1, n)
    ts = ts_ref[0]

    def weight_copy(layer, k):
        src, dst = ((win_hbm, win), (wout_hbm, wout), (wq_hbm, wq), (wm_hbm, wm), (wg_hbm, wg))[k]
        return pltpu.make_async_copy(src.at[layer], dst.at[layer], wsem.at[layer, k])

    for layer in range(LAYERS):
        for k in range(5):
            weight_copy(layer, k).start()

    barrier = pltpu.get_barrier_semaphore()

    def greet(k, c):
        pl.semaphore_signal(
            barrier, inc=1, device_id={"frames": lax.rem(me + k, n)}, device_id_type=MESH
        )
        return c

    lax.fori_loop(1, n, greet, 0)

    out_ref[...] = x_ref[...].astype(F32)
    tri[...] = jnp.where(iota((SPAN, SPAN), 0) >= iota((SPAN, SPAN), 1), 1.0, 0.0).astype(F32)
    lane_k = iota((LANES, INNER), 0)
    lane_j = iota((LANES, INNER), 1)
    expand[...] = jnp.where(
        (lane_k < 3 * HEADS) & (lax.rem(lane_k, HEADS) == lane_j // HEAD_DIM), 1.0, 0.0
    ).astype(BF16)
    half_a = iota((LANES, LANES), 0) // HEAD_DIM
    half_b = iota((LANES, LANES), 1) // HEAD_DIM
    ones[...] = jnp.where(half_a == half_b, 1.0, 0.0).astype(BF16)
    key_col = iota((tok, rows), 1) // tok
    for f in range(WINDOW):
        reach = lb_ref[f]
        own = (key_col <= f) & (key_col >= f - reach)
        prev = (key_col - WINDOW >= f - reach) & (me > 0)
        bias[f * tok : (f + 1) * tok, 0:rows] = jnp.where(own, 0.0, -1e30)
        bias[f * tok : (f + 1) * tok, rows : 2 * rows] = jnp.where(prev, 0.0, -1e30)
    spread = jnp.where(
        iota((HEADS, LANES), 0) == lax.rem(iota((HEADS, LANES), 1), HEADS), 1.0, 0.0
    ).astype(F32)

    def widen(x):
        group = iota(x.shape, 1) // HEADS
        hi = x.astype(BF16).astype(F32)
        rest = x - hi
        mid = rest.astype(BF16).astype(F32)
        low = rest - mid
        packed = jnp.where(group == 0, hi, jnp.where(group == 1, mid, jnp.where(group == 2, low, 0.0)))
        return packed.astype(BF16)

    def repeat_heads(row):
        return jnp.dot(row, spread, precision=HIGH, preferred_element_type=F32)

    def modulate(src, dst, shift, scale):
        for c in range(spans):
            v = src[c * SPAN : (c + 1) * SPAN, :]
            inv = lax.rsqrt(jnp.mean(v * v, axis=-1, keepdims=True) + EPS)
            dst[c * SPAN : (c + 1) * SPAN, :] = ((v * inv) * (1.0 + scale) + shift).astype(BF16)

    def tail_copy(layer):
        return pltpu.make_async_remote_copy(
            src_ref=tsend.at[layer], dst_ref=trecv.at[layer], send_sem=tss.at[layer],
            recv_sem=tsr.at[layer], device_id={"frames": nxt}, device_id_type=MESH,
        )

    def rows_copy(layer):
        return pltpu.make_async_remote_copy(
            src_ref=asend.at[layer], dst_ref=arecv.at[layer], send_sem=ass.at[layer],
            recv_sem=asr.at[layer], device_id={"frames": nxt}, device_id_type=MESH,
        )

    def gather_copy(layer, to, slot):
        return pltpu.make_async_remote_copy(
            src_ref=s1.at[layer, to], dst_ref=r1.at[layer, slot], send_sem=s1s.at[layer, to],
            recv_sem=s1r.at[layer, slot], device_id={"frames": to}, device_id_type=MESH,
        )

    def return_copy(layer, to, slot):
        return pltpu.make_async_remote_copy(
            src_ref=s2.at[layer, to], dst_ref=r2.at[layer, slot], send_sem=s2s.at[layer, to],
            recv_sem=s2r.at[layer, slot], device_id={"frames": to}, device_id_type=MESH,
        )

    def each_peer(fn):
        def step(k, c):
            fn(lax.rem(me + k, n))
            return c

        lax.fori_loop(1, n, step, 0)

    pl.semaphore_wait(barrier, n - 1)

    first = iota((SPAN, LANES), 1) < HEAD_DIM

    def block(layer, carry):
        mods = mod_ref[layer, ts].astype(F32)
        modulate(out_ref, ubuf, mods[0:1, :], mods[1:2, :])
        weight_copy(layer, 0).wait()
        u = ubuf[...]
        mixed_cols = INNER + 2 * STATE
        for c in range(0, mixed_cols, 256):
            res = mm(u, win[layer, :, INNER + c : INNER + c + 256]).astype(BF16)
            ext[8 : 8 + rows, c : c + 256] = res.astype(F32)
            tsend[layer, :, c : c + 256] = res[rows - 16 :, :]
        tail_copy(layer).start()
        wstep = mm(ws_ref[layer], spread.astype(BF16)).astype(BF16)
        raw = mm(u, wstep) + repeat_heads(sbias_ref[layer, pl.ds(ts, 1), :])
        step = jnp.maximum(raw, 0.0) + jnp.log1p(jnp.exp(-jnp.abs(raw)))
        logd = -jnp.exp(repeat_heads(dlog_ref[pl.ds(layer, 1), :])) * step
        cums = [
            jnp.dot(tri[...], logd[c * SPAN : (c + 1) * SPAN, :], precision=HIGH, preferred_element_type=F32)
            for c in range(spans)
        ]
        steps = [step[c * SPAN : (c + 1) * SPAN, :] for c in range(spans)]
        tail_copy(layer).wait_recv()
        for c in range(0, mixed_cols, 256):
            got = trecv[layer, :, c : c + 256].astype(F32)
            ext[0:8, c : c + 256] = jnp.where(me > 0, got[8:16, :], 0.0)
        taps = conv_ref[layer]
        for c in reversed(range(0, mixed_cols, LANES)):
            for r in range(spans):
                base = 8 - (CONV - 1) + r * SPAN
                total = taps[0:1, c : c + LANES] * ext[base : base + SPAN, c : c + LANES]
                for k in range(1, CONV):
                    total = total + taps[k : k + 1, c : c + LANES] * ext[
                        base + k : base + k + SPAN, c : c + LANES
                    ]
                act[r * SPAN : (r + 1) * SPAN, c : c + LANES] = (total * sigmoid(total)).astype(BF16)
        ends = [cum[SPAN - 1 : SPAN, :] for cum in cums]
        in_map = [act[c * SPAN : (c + 1) * SPAN, INNER : INNER + STATE] for c in range(spans)]
        out_map = [act[c * SPAN : (c + 1) * SPAN, INNER + STATE :] for c in range(spans)]
        in_t = [m.astype(F32).T.astype(BF16) for m in in_map]
        edges = [widen(jnp.exp(ends[c] - cums[c]) * steps[c]) for c in range(spans)]
        end_rows = [widen(jnp.broadcast_to(jnp.exp(e), (16, LANES))) for e in ends]
        befores = []
        for p in range(PAIRS):
            cols = slice(p * LANES, (p + 1) * LANES)
            state = None
            decay = None
            for c in range(spans):
                scaled = act[c * SPAN : (c + 1) * SPAN, cols].astype(F32) * mm(edges[c], expand[:, cols])
                term = mm(in_t[c], scaled.astype(BF16))
                row = mm(end_rows[c], expand[:, cols])
                if state is None:
                    state, decay = term, row
                else:
                    yloc[c * SPAN : (c + 1) * SPAN, cols] = mm(out_map[c], state.astype(BF16))
                    state = row[0:1, :] * state + term
                    decay = row * decay
            per = n // PAIRS
            for k in range(per):
                s1[layer, p * per + k, 0:part, :] = state[k * part : (k + 1) * part, :].astype(BF16)
                s1[layer, p * per + k, part:, :] = decay.astype(BF16)
        each_peer(lambda to: gather_copy(layer, to, me).start())
        r1[layer, me] = s1[layer, me]

        for c in range(0, INNER, 256):
            gate[:, c : c + 256] = mm(u, win[layer, :, c : c + 256]).astype(BF16)
        lower = iota((SPAN, SPAN), 0) >= iota((SPAN, SPAN), 1)
        grow = [None] * spans
        reach_end = None
        for c in range(spans):
            span = slice(c * SPAN, (c + 1) * SPAN)
            cum, cum_t, step_t = cums[c], cums[c].T, steps[c].T
            affinity = jnp.where(lower, mm_t(out_map[c], in_map[c]), 0.0)
            inner_grow = widen(jnp.exp(cum))
            total_log = cum if reach_end is None else cum + reach_end
            grow[c] = widen(jnp.exp(total_log))
            reach_end = ends[c] if reach_end is None else reach_end + ends[c]
            for p in range(PAIRS):
                cols = slice(p * LANES, (p + 1) * LANES)
                values = act[span, cols]
                outs = []
                for h in (2 * p, 2 * p + 1):
                    gaps = jnp.minimum(cum[:, h : h + 1] - cum_t[h : h + 1, :], 0.0)
                    mixing = (affinity * jnp.exp(gaps) * step_t[h : h + 1, :]).astype(BF16)
                    outs.append(mm(mixing, values))
                y = jnp.where(first, outs[0], outs[1])
                if c > 0:
                    y = y + yloc[span, cols] * mm(inner_grow, expand[:, cols])
                yloc[span, cols] = y

        each_peer(lambda frm: gather_copy(layer, frm, frm).wait_recv())
        run = jnp.zeros((part, LANES), F32)
        for k in range(n):
            s2[layer, k] = run.astype(BF16)
            run = r1[layer, k, part : part + 1, :].astype(F32) * run + r1[layer, k, 0:part, :].astype(F32)
        each_peer(lambda to: return_copy(layer, to, me).start())
        r2[layer, me] = s2[layer, me]
        skip_row = widen(repeat_heads(jnp.broadcast_to(skip_ref[pl.ds(layer, 1), :], (16, HEADS))))
        for p in range(PAIRS):
            cols = slice(p * LANES, (p + 1) * LANES)
            skip = mm(skip_row, expand[:, cols])[0:1, :]
            yloc[:, cols] = yloc[:, cols] + skip * act[:, cols].astype(F32)
        each_peer(lambda frm: return_copy(layer, frm, frm).wait_recv())

        gain = gain_ref[pl.ds(layer, 1), :]
        per = n // PAIRS
        for p in range(PAIRS):
            cols = slice(p * LANES, (p + 1) * LANES)
            incoming = r2[layer, p * per : (p + 1) * per].reshape(STATE, LANES)
            for c in range(spans):
                span = slice(c * SPAN, (c + 1) * SPAN)
                carried = mm(out_map[c], incoming) * mm(grow[c], expand[:, cols])
                y = yloc[span, cols] + carried
                z = gate[span, cols].astype(F32)
                g = y * (z * sigmoid(z))
                sq = g * g
                hi = sq.astype(BF16)
                lo = (sq - hi.astype(F32)).astype(BF16)
                ms = (mm(hi, ones[...]) + mm(lo, ones[...])) * (1.0 / HEAD_DIM)
                gbuf[span, cols] = (g * lax.rsqrt(ms + HEAD_EPS) * gain[:, cols]).astype(BF16)
        weight_copy(layer, 1).wait()
        g_all = gbuf[...]
        for c in range(0, width, 256):
            hid[:, c : c + 256] = out_ref[:, c : c + 256] + mm(g_all, wout[layer, :, c : c + 256])
        modulate(hid, asend.at[layer], mods[2:3, :], mods[3:4, :])
        rows_copy(layer).start()
        weight_copy(layer, 2).wait()
        weight_copy(layer, 3).wait()
        a = asend[layer]
        for c in range(0, ATTN, 256):
            q = mm(a, wq[layer, :, c : c + 256]).astype(BF16)
            qb[:, c : c + 256] = (q.astype(F32) * HEAD_DIM ** (-0.5)).astype(BF16)
        for c in range(0, 2 * ATTN, 256):
            kv[:, c : c + 256] = mm(a, wm[layer, :, c : c + 256]).astype(BF16)

        def attend_half(p, h, span, keys, cols, shift):
            q = qb[span, cols]
            mine = first if h == 0 else ~first
            q = jnp.where(mine, q, jnp.zeros_like(q))
            s = mm_t(q, keys[:, cols]) + bias[span, shift : shift + rows]
            top = jnp.max(s, axis=-1, keepdims=True)
            w = jnp.exp(s - top)
            total = jnp.sum(w, axis=-1, keepdims=True)
            vals = keys[:, ATTN + p * LANES : ATTN + (p + 1) * LANES]
            return top, total, mm(w.astype(BF16), vals)

        for p in range(ATTN // LANES):
            cols = slice(p * LANES, (p + 1) * LANES)
            for c in range(spans):
                span = slice(c * SPAN, (c + 1) * SPAN)
                o = []
                for h in range(2):
                    top, total, mixed = attend_half(p, h, span, kv, cols, 0)
                    idx = 2 * p + h
                    mstat[span, idx : idx + 1] = top
                    lstat[span, idx : idx + 1] = total
                    o.append(mixed)
                oacc[span, cols] = jnp.where(first, o[0], o[1])
        rows_copy(layer).wait_recv()
        a = arecv[layer]
        for c in range(0, 2 * ATTN, 256):
            kvp[:, c : c + 256] = mm(a, wm[layer, :, c : c + 256]).astype(BF16)
        for p in range(ATTN // LANES):
            cols = slice(p * LANES, (p + 1) * LANES)
            for c in range(spans):
                span = slice(c * SPAN, (c + 1) * SPAN)
                o, fa, fb = [], [], []
                for h in range(2):
                    top, total, mixed = attend_half(p, h, span, kvp, cols, rows)
                    idx = 2 * p + h
                    top0, total0 = mstat[span, idx : idx + 1], lstat[span, idx : idx + 1]
                    most = jnp.maximum(top, top0)
                    wa, wb = jnp.exp(top0 - most), jnp.exp(top - most)
                    inv = 1.0 / (wa * total0 + wb * total)
                    o.append(mixed)
                    fa.append(wa * inv)
                    fb.append(wb * inv)
                res = oacc[span, cols] * jnp.where(first, fa[0], fa[1]) + jnp.where(
                    first, o[0] * fb[0], o[1] * fb[1]
                )
                gbuf[span, cols] = res.astype(BF16)
        weight_copy(layer, 4).wait()
        att = gbuf[:, 0:ATTN]
        for c in range(0, width, 256):
            out_ref[:, c : c + 256] = hid[:, c : c + 256] + mm(att, wg[layer, :, c : c + 256])
        tail_copy(layer).wait_send()
        rows_copy(layer).wait_send()
        each_peer(lambda to: gather_copy(layer, to, me).wait_send())
        each_peer(lambda to: return_copy(layer, to, me).wait_send())
        return carry

    lax.fori_loop(0, LAYERS, block, 0)


def shards(
    n, latents, timestep, lookback, modulation, input_weight, step_weight, conv_weight, step_bias,
    decay_log, skip_gain, norm_gain, output_weight, query_weight, memory_weight, merge_weight,
):
    frames_dev, tok, width = latents.shape
    rows = frames_dev * tok
    part = INNER * STATE // n // LANES
    vmem = pl.BlockSpec(memory_space=pltpu.VMEM)
    smem = pl.BlockSpec(memory_space=pltpu.SMEM)
    hbm = pl.BlockSpec(memory_space=pl.ANY)
    mixed_cols = INNER + 2 * STATE
    dma = pltpu.SemaphoreType.DMA
    out = pl.pallas_call(
        functools.partial(kernel, n),
        out_shape=jax.ShapeDtypeStruct((rows, width), F32),
        in_specs=[
            vmem, smem, smem, vmem, hbm, vmem, vmem, vmem, vmem, vmem, vmem, hbm, hbm, hbm, hbm,
        ],
        out_specs=vmem,
        scratch_shapes=[
            pltpu.VMEM(input_weight.shape, BF16),
            pltpu.VMEM(output_weight.shape, BF16),
            pltpu.VMEM(query_weight.shape, BF16),
            pltpu.VMEM(memory_weight.shape, BF16),
            pltpu.VMEM(merge_weight.shape, BF16),
            dma((LAYERS, 5)),
            pltpu.VMEM((rows, width), F32),
            pltpu.VMEM((rows, width), BF16),
            pltpu.VMEM((rows, INNER), BF16),
            pltpu.VMEM((rows + 8, mixed_cols), F32),
            pltpu.VMEM((rows, mixed_cols), BF16),
            pltpu.VMEM((rows, INNER), F32),
            pltpu.VMEM((rows, INNER), BF16),
            pltpu.VMEM((SPAN, SPAN), F32),
            pltpu.VMEM((LANES, INNER), BF16),
            pltpu.VMEM((rows, 2 * rows), F32),
            pltpu.VMEM((LANES, LANES), BF16),
            pltpu.VMEM((LAYERS, n, part + 16, LANES), BF16),
            pltpu.VMEM((LAYERS, n, part + 16, LANES), BF16),
            pltpu.VMEM((LAYERS, n, part, LANES), BF16),
            pltpu.VMEM((LAYERS, n, part, LANES), BF16),
            dma((LAYERS, n)), dma((LAYERS, n)), dma((LAYERS, n)), dma((LAYERS, n)),
            pltpu.VMEM((LAYERS, 16, mixed_cols), BF16),
            pltpu.VMEM((LAYERS, 16, mixed_cols), BF16),
            dma((LAYERS,)), dma((LAYERS,)),
            pltpu.VMEM((LAYERS, rows, width), BF16),
            pltpu.VMEM((LAYERS, rows, width), BF16),
            dma((LAYERS,)), dma((LAYERS,)),
            pltpu.VMEM((rows, ATTN), BF16),
            pltpu.VMEM((rows, 2 * ATTN), BF16),
            pltpu.VMEM((rows, 2 * ATTN), BF16),
            pltpu.VMEM((rows, ATTN), F32),
            pltpu.VMEM((rows, LANES), F32),
            pltpu.VMEM((rows, LANES), F32),
        ],
        compiler_params=pltpu.CompilerParams(
            collective_id=0, has_side_effects=True, vmem_limit_bytes=56 * 1024 * 1024
        ),
    )(
        latents.reshape(rows, width), timestep, lookback, modulation, input_weight, step_weight,
        conv_weight, step_bias, decay_log, skip_gain, norm_gain, output_weight, query_weight,
        memory_weight, merge_weight,
    )
    return out.reshape(latents.shape)


def solution(mesh):
    split = P(("groups", "frames"))
    frames = P(("groups", "frames"), None, None)
    return jax.shard_map(
        functools.partial(shards, mesh.shape["frames"]),
        mesh=mesh,
        in_specs=(frames, split, split) + (P(),) * 12,
        out_specs=frames,
        check_vma=False,
    )
```

time: 267 us -> 79 us (0.30)
  the two profiles are of different devices: /device:TPU:8 before, /device:TPU:0 now
where the time goes in v1:
time: 79 us; the launch traced here: 78.7 us
  Pallas kernels  73.8 us (93%)
  local copies, waits for them, and re-layouts  4.89 us (6%)
    pallas_call x1, Pallas kernels, shards(): pl.pallas_call(functools.partial(kernel, n), out_shape=jax.ShapeDtypeStru...  73.8 us
    unnamed x3, local copies, waits for them, and re-layouts  4.89 us

profile of v1, /device:TPU:0, one launch (start us, length us, event | category | flops | bytes accessed | tf_op | source)
XLA Modules:
  0.0 78.7 jit_solution(7015823366416643594)
XLA Ops:
  0.0 1.4 %copy.17.sbias_ref = f32[2,50,16]{2,1,0:T(8,128)} copy(f32[2,50,16]{1,2,0:T(8,128)} %param.22) | data formatting | bytes 12800 | tf_op args[7]
  1.4 1.6 %copy.16.ws_ref = bf16[2,512,16]{2,1,0:T(8,128)(2,1)} copy(bf16[2,512,16]{1,2,0:T(8,128)(2,1)} %param.20) | data formatting | bytes 65536 | tf_op args[5]
  3.0 73.8 %shard_map.145 = f32[256,512]{1,0:T(8,128)} custom-call(bf16[256,512]{1,0:T(8,128)(2,1)} %bitcast.3, s32[8]{0:T(128)} %ts_ref.1, s32[8]{0:T(128)} %lb_ref.1, bf16[2,50,4,512]{3,2,1,0:T(4,128)(2,1)} %mod_ref.1, bf16[2,512,2304]{2,1,0:T(8,128)(2,1)} %win_hbm.1, bf16[2,512,16]{2,1,0:T(8,128)(2,1)} %copy.16.ws_ref, f32[2,4,1280]{2,1,0:T(4,128)} %conv_ref.1, ...), custom_call_target="tpu_custom_call" | custom-call | tf_op jit(solution)/shard_map/pallas_call | solution.py:361
  76.9 1.9 %copy.19 = f32[8,32,512]{2,1,0:T(8,128)} copy(f32[8,32,512]{2,1,0:T(8,128)} %bitcast.2) | data formatting | bytes 1048576

commit v2 on v1

--- a/solution.py
+++ b/solution.py
@@ -50,15 +50,19 @@
     out_ref,
     win, wout, wq, wm, wg, wsem,
     hid, ubuf, gate, ext, act, yloc, gbuf, tri, expand, bias, ones,
-    s1, r1, s2, r2, s1s, s1r, s2s, s2r,
+    s1, r1, s2, r2, s1s, s1r, s2s, s2r, cin, cout, cs, cr,
     tsend, trecv, tss, tsr, asend, arecv, ass, asr,
     qb, kv, kvp, oacc, mstat, lstat,
 ):
     rows, width = x_ref.shape
     spans = rows // SPAN
     tok = rows // WINDOW
-    part = r2.shape[2]
     me = lax.axis_index("frames")
+    team = PAIRS
+    teams = n // team
+    mine_team = me // team
+    lid = lax.rem(me, team)
+    base_id = mine_team * team
     nxt = lax.rem(me + 1, n)
     ts = ts_ref[0]
 
@@ -113,8 +117,8 @@
     def repeat_heads(row):
         return jnp.dot(row, spread, precision=HIGH, preferred_element_type=F32)
 
-    def modulate(src, dst, shift, scale):
-        for c in range(spans):
+    def modulate(src, dst, shift, scale, which):
+        for c in which:
             v = src[c * SPAN : (c + 1) * SPAN, :]
             inv = lax.rsqrt(jnp.mean(v * v, axis=-1, keepdims=True) + EPS)
             dst[c * SPAN : (c + 1) * SPAN, :] = ((v * inv) * (1.0 + scale) + shift).astype(BF16)
@@ -125,38 +129,45 @@
             recv_sem=tsr.at[layer], device_id={"frames": nxt}, device_id_type=MESH,
         )
 
-    def rows_copy(layer):
+    def rows_copy(layer, c):
+        span = pl.ds(c * SPAN, SPAN)
         return pltpu.make_async_remote_copy(
-            src_ref=asend.at[layer], dst_ref=arecv.at[layer], send_sem=ass.at[layer],
-            recv_sem=asr.at[layer], device_id={"frames": nxt}, device_id_type=MESH,
-        )
-
-    def gather_copy(layer, to, slot):
+            src_ref=asend.at[layer, span], dst_ref=arecv.at[layer, span], send_sem=ass.at[layer, c],
+            recv_sem=asr.at[layer, c], device_id={"frames": nxt}, device_id_type=MESH,
+        )
+
+    def gather_copy(layer, owner, slot):
         return pltpu.make_async_remote_copy(
-            src_ref=s1.at[layer, to], dst_ref=r1.at[layer, slot], send_sem=s1s.at[layer, to],
-            recv_sem=s1r.at[layer, slot], device_id={"frames": to}, device_id_type=MESH,
+            src_ref=s1.at[layer, owner], dst_ref=r1.at[layer, slot], send_sem=s1s.at[layer, owner],
+            recv_sem=s1r.at[layer, slot], device_id={"frames": base_id + owner}, device_id_type=MESH,
         )
 
     def return_copy(layer, to, slot):
         return pltpu.make_async_remote_copy(
             src_ref=s2.at[layer, to], dst_ref=r2.at[layer, slot], send_sem=s2s.at[layer, to],
-            recv_sem=s2r.at[layer, slot], device_id={"frames": to}, device_id_type=MESH,
-        )
-
-    def each_peer(fn):
-        def step(k, c):
-            fn(lax.rem(me + k, n))
-            return c
-
-        lax.fori_loop(1, n, step, 0)
-
-    pl.semaphore_wait(barrier, n - 1)
+            recv_sem=s2r.at[layer, slot], device_id={"frames": base_id + to}, device_id_type=MESH,
+        )
+
+    def chain_copy(layer):
+        return pltpu.make_async_remote_copy(
+            src_ref=cout.at[layer], dst_ref=cin.at[layer], send_sem=cs.at[layer],
+            recv_sem=cr.at[layer], device_id={"frames": lax.rem(me + team, n)}, device_id_type=MESH,
+        )
+
+    def unless_me(k, fn):
+        @pl.when(lid != k)
+        def _():
+            fn()
+
+    @pl.when(mine_team == 0)
+    def _():
+        cin[...] = jnp.zeros_like(cin)
 
     first = iota((SPAN, LANES), 1) < HEAD_DIM
 
     def block(layer, carry):
         mods = mod_ref[layer, ts].astype(F32)
-        modulate(out_ref, ubuf, mods[0:1, :], mods[1:2, :])
+        modulate(out_ref, ubuf, mods[0:1, :], mods[1:2, :], range(spans))
         weight_copy(layer, 0).wait()
         u = ubuf[...]
         mixed_cols = INNER + 2 * STATE
@@ -164,9 +175,21 @@
             res = mm(u, win[layer, :, INNER + c : INNER + c + 256]).astype(BF16)
             ext[8 : 8 + rows, c : c + 256] = res.astype(F32)
             tsend[layer, :, c : c + 256] = res[rows - 16 :, :]
+
+        @pl.when(layer == 0)
+        def _():
+            pl.semaphore_wait(barrier, n - 1)
+
         tail_copy(layer).start()
-        wstep = mm(ws_ref[layer], spread.astype(BF16)).astype(BF16)
-        raw = mm(u, wstep) + repeat_heads(sbias_ref[layer, pl.ds(ts, 1), :])
+        for c in range(0, INNER, 256):
+            gate[:, c : c + 256] = mm(u, win[layer, :, c : c + 256]).astype(BF16)
+        wstep = lax.dot_general(
+            spread.astype(BF16), ws_ref[layer], (((0,), (0,)), ((), ())), preferred_element_type=F32
+        ).astype(BF16)
+        sbias = sbias_ref[layer]
+        here = jnp.where(iota(sbias.shape, 1) == ts, sbias, 0.0)
+        here = jnp.sum(jnp.sum(here, axis=-1, keepdims=True) * spread, axis=0, keepdims=True)
+        raw = mm_t(u, wstep) + here
         step = jnp.maximum(raw, 0.0) + jnp.log1p(jnp.exp(-jnp.abs(raw)))
         logd = -jnp.exp(repeat_heads(dlog_ref[pl.ds(layer, 1), :])) * step
         cums = [
@@ -174,14 +197,15 @@
             for c in range(spans)
         ]
         steps = [step[c * SPAN : (c + 1) * SPAN, :] for c in range(spans)]
-        tail_copy(layer).wait_recv()
-        for c in range(0, mixed_cols, 256):
-            got = trecv[layer, :, c : c + 256].astype(F32)
-            ext[0:8, c : c + 256] = jnp.where(me > 0, got[8:16, :], 0.0)
         taps = conv_ref[layer]
-        for c in reversed(range(0, mixed_cols, LANES)):
-            for r in range(spans):
-                base = 8 - (CONV - 1) + r * SPAN
+        for r in reversed(range(spans)):
+            if r == 0:
+                tail_copy(layer).wait_recv()
+                for c in range(0, mixed_cols, 256):
+                    got = trecv[layer, :, c : c + 256].astype(F32)
+                    ext[0:8, c : c + 256] = jnp.where(me > 0, got[8:16, :], 0.0)
+            base = 8 - (CONV - 1) + r * SPAN
+            for c in range(0, mixed_cols, LANES):
                 total = taps[0:1, c : c + LANES] * ext[base : base + SPAN, c : c + LANES]
                 for k in range(1, CONV):
                     total = total + taps[k : k + 1, c : c + LANES] * ext[
@@ -209,15 +233,11 @@
                     yloc[c * SPAN : (c + 1) * SPAN, cols] = mm(out_map[c], state.astype(BF16))
                     state = row[0:1, :] * state + term
                     decay = row * decay
-            per = n // PAIRS
-            for k in range(per):
-                s1[layer, p * per + k, 0:part, :] = state[k * part : (k + 1) * part, :].astype(BF16)
-                s1[layer, p * per + k, part:, :] = decay.astype(BF16)
-        each_peer(lambda to: gather_copy(layer, to, me).start())
-        r1[layer, me] = s1[layer, me]
-
-        for c in range(0, INNER, 256):
-            gate[:, c : c + 256] = mm(u, win[layer, :, c : c + 256]).astype(BF16)
+            s1[layer, p, 0:STATE, :] = state.astype(BF16)
+            s1[layer, p, STATE:, :] = decay.astype(BF16)
+            unless_me(p, lambda: gather_copy(layer, p, lid).start())
+        r1[layer, lid] = s1[layer, lid]
+
         lower = iota((SPAN, SPAN), 0) >= iota((SPAN, SPAN), 1)
         grow = [None] * spans
         reach_end = None
@@ -242,25 +262,43 @@
                     y = y + yloc[span, cols] * mm(inner_grow, expand[:, cols])
                 yloc[span, cols] = y
 
-        each_peer(lambda frm: gather_copy(layer, frm, frm).wait_recv())
-        run = jnp.zeros((part, LANES), F32)
-        for k in range(n):
-            s2[layer, k] = run.astype(BF16)
-            run = r1[layer, k, part : part + 1, :].astype(F32) * run + r1[layer, k, 0:part, :].astype(F32)
-        each_peer(lambda to: return_copy(layer, to, me).start())
-        r2[layer, me] = s2[layer, me]
+        run = jnp.zeros((STATE, LANES), F32)
+        whole = jnp.ones((1, LANES), F32)
+        for k in range(team):
+            unless_me(k, lambda: gather_copy(layer, k, k).wait_recv())
+            decay = r1[layer, k, STATE : STATE + 1, :].astype(F32)
+            run = decay * run + r1[layer, k, 0:STATE, :].astype(F32)
+            whole = whole * decay
+
+        @pl.when(mine_team > 0)
+        def _():
+            chain_copy(layer).wait_recv()
+
+        before = cin[layer].astype(F32)
+        cout[layer] = (whole * before + run).astype(BF16)
+
+        @pl.when(mine_team < teams - 1)
+        def _():
+            chain_copy(layer).start()
+
+        for k in range(team):
+            s2[layer, k] = before.astype(BF16)
+            unless_me(k, lambda: return_copy(layer, k, lid).start())
+            before = r1[layer, k, STATE : STATE + 1, :].astype(F32) * before + r1[
+                layer, k, 0:STATE, :
+            ].astype(F32)
+        r2[layer, lid] = s2[layer, lid]
         skip_row = widen(repeat_heads(jnp.broadcast_to(skip_ref[pl.ds(layer, 1), :], (16, HEADS))))
         for p in range(PAIRS):
             cols = slice(p * LANES, (p + 1) * LANES)
             skip = mm(skip_row, expand[:, cols])[0:1, :]
             yloc[:, cols] = yloc[:, cols] + skip * act[:, cols].astype(F32)
-        each_peer(lambda frm: return_copy(layer, frm, frm).wait_recv())
 
         gain = gain_ref[pl.ds(layer, 1), :]
-        per = n // PAIRS
         for p in range(PAIRS):
             cols = slice(p * LANES, (p + 1) * LANES)
-            incoming = r2[layer, p * per : (p + 1) * per].reshape(STATE, LANES)
+            unless_me(p, lambda: return_copy(layer, p, p).wait_recv())
+            incoming = r2[layer, p]
             for c in range(spans):
                 span = slice(c * SPAN, (c + 1) * SPAN)
                 carried = mm(out_map[c], incoming) * mm(grow[c], expand[:, cols])
@@ -273,11 +311,14 @@
                 ms = (mm(hi, ones[...]) + mm(lo, ones[...])) * (1.0 / HEAD_DIM)
                 gbuf[span, cols] = (g * lax.rsqrt(ms + HEAD_EPS) * gain[:, cols]).astype(BF16)
         weight_copy(layer, 1).wait()
-        g_all = gbuf[...]
-        for c in range(0, width, 256):
-            hid[:, c : c + 256] = out_ref[:, c : c + 256] + mm(g_all, wout[layer, :, c : c + 256])
-        modulate(hid, asend.at[layer], mods[2:3, :], mods[3:4, :])
-        rows_copy(layer).start()
+        for r in range(spans):
+            span = slice(r * SPAN, (r + 1) * SPAN)
+            for c in range(0, width, 256):
+                hid[span, c : c + 256] = out_ref[span, c : c + 256] + mm(
+                    gbuf[span, :], wout[layer, :, c : c + 256]
+                )
+            modulate(hid, asend.at[layer], mods[2:3, :], mods[3:4, :], [r])
+            rows_copy(layer, r).start()
         weight_copy(layer, 2).wait()
         weight_copy(layer, 3).wait()
         a = asend[layer]
@@ -287,30 +328,34 @@
         for c in range(0, 2 * ATTN, 256):
             kv[:, c : c + 256] = mm(a, wm[layer, :, c : c + 256]).astype(BF16)
 
-        def attend_half(p, h, span, keys, cols, shift):
-            q = qb[span, cols]
-            mine = first if h == 0 else ~first
-            q = jnp.where(mine, q, jnp.zeros_like(q))
-            s = mm_t(q, keys[:, cols]) + bias[span, shift : shift + rows]
-            top = jnp.max(s, axis=-1, keepdims=True)
-            w = jnp.exp(s - top)
-            total = jnp.sum(w, axis=-1, keepdims=True)
-            vals = keys[:, ATTN + p * LANES : ATTN + (p + 1) * LANES]
-            return top, total, mm(w.astype(BF16), vals)
+        def attend(p, span, keys, lo, hi, shift):
+            cols = slice(p * LANES, (p + 1) * LANES)
+            q, k = qb[span, cols], keys[lo:hi, cols]
+            vals = keys[lo:hi, ATTN + p * LANES : ATTN + (p + 1) * LANES]
+            lanes = iota(vals.shape, 1) < HEAD_DIM
+            tops, mixes = [], []
+            for h in range(2):
+                mine = first if h == 0 else ~first
+                s = mm_t(jnp.where(mine, q, jnp.zeros_like(q)), k) + bias[span, shift + lo : shift + hi]
+                top = jnp.max(s, axis=-1, keepdims=True)
+                mine = lanes if h == 0 else ~lanes
+                w = jnp.exp(s - top).astype(BF16)
+                mixes.append(mm(w, jnp.where(mine, vals, jnp.ones_like(vals))))
+                tops.append(top)
+            top = jnp.where(first, tops[0], tops[1])
+            total = pltpu.roll(jnp.where(first, mixes[1], mixes[0]), HEAD_DIM, 1)
+            return top, total, jnp.where(first, mixes[0], mixes[1])
 
         for p in range(ATTN // LANES):
             cols = slice(p * LANES, (p + 1) * LANES)
             for c in range(spans):
                 span = slice(c * SPAN, (c + 1) * SPAN)
-                o = []
-                for h in range(2):
-                    top, total, mixed = attend_half(p, h, span, kv, cols, 0)
-                    idx = 2 * p + h
-                    mstat[span, idx : idx + 1] = top
-                    lstat[span, idx : idx + 1] = total
-                    o.append(mixed)
-                oacc[span, cols] = jnp.where(first, o[0], o[1])
-        rows_copy(layer).wait_recv()
+                top, total, mixed = attend(p, span, kv, 0, (c + 1) * SPAN, 0)
+                mstat[span, cols] = top
+                lstat[span, cols] = total
+                oacc[span, cols] = mixed
+        for c in range(spans):
+            rows_copy(layer, c).wait_recv()
         a = arecv[layer]
         for c in range(0, 2 * ATTN, 256):
             kvp[:, c : c + 256] = mm(a, wm[layer, :, c : c + 256]).astype(BF16)
@@ -318,29 +363,27 @@
             cols = slice(p * LANES, (p + 1) * LANES)
             for c in range(spans):
                 span = slice(c * SPAN, (c + 1) * SPAN)
-                o, fa, fb = [], [], []
-                for h in range(2):
-                    top, total, mixed = attend_half(p, h, span, kvp, cols, rows)
-                    idx = 2 * p + h
-                    top0, total0 = mstat[span, idx : idx + 1], lstat[span, idx : idx + 1]
-                    most = jnp.maximum(top, top0)
-                    wa, wb = jnp.exp(top0 - most), jnp.exp(top - most)
-                    inv = 1.0 / (wa * total0 + wb * total)
-                    o.append(mixed)
-                    fa.append(wa * inv)
-                    fb.append(wb * inv)
-                res = oacc[span, cols] * jnp.where(first, fa[0], fa[1]) + jnp.where(
-                    first, o[0] * fb[0], o[1] * fb[1]
-                )
-                gbuf[span, cols] = res.astype(BF16)
+                top, total, mixed = attend(p, span, kvp, c * SPAN, rows, rows)
+                top0 = mstat[span, cols]
+                most = jnp.maximum(top, top0)
+                wa, wb = jnp.exp(top0 - most), jnp.exp(top - most)
+                inv = 1.0 / (wa * lstat[span, cols] + wb * total)
+                gbuf[span, cols] = ((wa * oacc[span, cols] + wb * mixed) * inv).astype(BF16)
         weight_copy(layer, 4).wait()
         att = gbuf[:, 0:ATTN]
         for c in range(0, width, 256):
             out_ref[:, c : c + 256] = hid[:, c : c + 256] + mm(att, wg[layer, :, c : c + 256])
         tail_copy(layer).wait_send()
-        rows_copy(layer).wait_send()
-        each_peer(lambda to: gather_copy(layer, to, me).wait_send())
-        each_peer(lambda to: return_copy(layer, to, me).wait_send())
+        for c in range(spans):
+            rows_copy(layer, c).wait_send()
+        for k in range(team):
+            unless_me(k, lambda: gather_copy(layer, k, lid).wait_send())
+            unless_me(k, lambda: return_copy(layer, k, lid).wait_send())
+
+        @pl.when(mine_team < teams - 1)
+        def _():
+            chain_copy(layer).wait_send()
+
         return carry
 
     lax.fori_loop(0, LAYERS, block, 0)
@@ -352,7 +395,7 @@
 ):
     frames_dev, tok, width = latents.shape
     rows = frames_dev * tok
-    part = INNER * STATE // n // LANES
+    assert n % PAIRS == 0
     vmem = pl.BlockSpec(memory_space=pltpu.VMEM)
     smem = pl.BlockSpec(memory_space=pltpu.SMEM)
     hbm = pl.BlockSpec(memory_space=pl.ANY)
@@ -383,30 +426,33 @@
             pltpu.VMEM((LANES, INNER), BF16),
             pltpu.VMEM((rows, 2 * rows), F32),
             pltpu.VMEM((LANES, LANES), BF16),
-            pltpu.VMEM((LAYERS, n, part + 16, LANES), BF16),
-            pltpu.VMEM((LAYERS, n, part + 16, LANES), BF16),
-            pltpu.VMEM((LAYERS, n, part, LANES), BF16),
-            pltpu.VMEM((LAYERS, n, part, LANES), BF16),
-            dma((LAYERS, n)), dma((LAYERS, n)), dma((LAYERS, n)), dma((LAYERS, n)),
+            pltpu.VMEM((LAYERS, PAIRS, STATE + 16, LANES), BF16),
+            pltpu.VMEM((LAYERS, PAIRS, STATE + 16, LANES), BF16),
+            pltpu.VMEM((LAYERS, PAIRS, STATE, LANES), BF16),
+            pltpu.VMEM((LAYERS, PAIRS, STATE, LANES), BF16),
+            dma((LAYERS, PAIRS)), dma((LAYERS, PAIRS)), dma((LAYERS, PAIRS)), dma((LAYERS, PAIRS)),
+            pltpu.VMEM((LAYERS, STATE, LANES), BF16),
+            pltpu.VMEM((LAYERS, STATE, LANES), BF16),
+            dma((LAYERS,)), dma((LAYERS,)),
             pltpu.VMEM((LAYERS, 16, mixed_cols), BF16),
             pltpu.VMEM((LAYERS, 16, mixed_cols), BF16),
             dma((LAYERS,)), dma((LAYERS,)),
             pltpu.VMEM((LAYERS, rows, width), BF16),
             pltpu.VMEM((LAYERS, rows, width), BF16),
-            dma((LAYERS,)), dma((LAYERS,)),
+            dma((LAYERS, rows // SPAN)), dma((LAYERS, rows // SPAN)),
             pltpu.VMEM((rows, ATTN), BF16),
             pltpu.VMEM((rows, 2 * ATTN), BF16),
             pltpu.VMEM((rows, 2 * ATTN), BF16),
             pltpu.VMEM((rows, ATTN), F32),
-            pltpu.VMEM((rows, LANES), F32),
-            pltpu.VMEM((rows, LANES), F32),
+            pltpu.VMEM((rows, ATTN), F32),
+            pltpu.VMEM((rows, ATTN), F32),
         ],
         compiler_params=pltpu.CompilerParams(
             collective_id=0, has_side_effects=True, vmem_limit_bytes=56 * 1024 * 1024
         ),
     )(
-        latents.reshape(rows, width), timestep, lookback, modulation, input_weight, step_weight,
-        conv_weight, step_bias, decay_log, skip_gain, norm_gain, output_weight, query_weight,
+        latents.reshape(rows, width), timestep, lookback, modulation, input_weight,
+        jnp.swapaxes(step_weight, 1, 2), conv_weight, jnp.swapaxes(step_bias, 1, 2), decay_log, skip_gain, norm_gain, output_weight, query_weight,
         memory_weight, merge_weight,
     )
     return out.reshape(latents.shape)

time: 79 us -> 68.2 us (0.86)
  Pallas kernels: 73.8 us -> 66.2 us
  local copies, waits for them, and re-layouts: 4.89 us -> 1.87 us
    pallas_call x1, Pallas kernels: 73.8 us -> 66.2 us  [shards(): pl.pallas_call(functools.partial(kernel, n), out_shape=jax.ShapeDtypeStru...]
    unnamed x3 -> x1, local copies, waits for them, and re-layouts: 4.89 us -> 1.87 us
where the time goes in v2:
time: 68.2 us; the launch traced here: 68 us
  Pallas kernels  66.2 us (97%)
  local copies, waits for them, and re-layouts  1.87 us (3%)
    pallas_call x1, Pallas kernels, shards(): pl.pallas_call(functools.partial(kernel, n), out_shape=jax.ShapeDtypeStru...  66.2 us
    unnamed x1, local copies, waits for them, and re-layouts  1.87 us

profile of v2, /device:TPU:0, one launch (start us, length us, event | category | flops | bytes accessed | tf_op | source)
XLA Modules:
  0.0 68.0 jit_solution(8343328126403531664)
XLA Ops:
  0.0 66.2 %shard_map.145 = f32[256,512]{1,0:T(8,128)} custom-call(bf16[256,512]{1,0:T(8,128)(2,1)} %bitcast.5, s32[8]{0:T(128)} %ts_ref.1, s32[8]{0:T(128)} %lb_ref.1, bf16[2,50,4,512]{3,2,1,0:T(4,128)(2,1)} %mod_ref.1, bf16[2,512,2304]{2,1,0:T(8,128)(2,1)} %win_hbm.1, bf16[2,16,512]{2,1,0:T(8,128)(2,1)} %bitcast.6, f32[2,4,1280]{2,1,0:T(4,128)} %conv_ref.1, ...), custom_call_target="tpu_custom_call" | custom-call | tf_op jit(solution)/shard_map/pallas_call | solution.py:404
  66.2 1.9 %copy.17 = f32[8,32,512]{2,1,0:T(8,128)} copy(f32[8,32,512]{2,1,0:T(8,128)} %bitcast.4) | data formatting | bytes 1048576

commit v3 on v2

--- a/solution.py
+++ b/solution.py
@@ -52,7 +52,7 @@
     hid, ubuf, gate, ext, act, yloc, gbuf, tri, expand, bias, ones,
     s1, r1, s2, r2, s1s, s1r, s2s, s2r, cin, cout, cs, cr,
     tsend, trecv, tss, tsr, asend, arecv, ass, asr,
-    qb, kv, kvp, oacc, mstat, lstat,
+    qb, kv, kvp, oacc, mstat, lstat, swish, growx,
 ):
     rows, width = x_ref.shape
     spans = rows // SPAN
@@ -153,6 +153,13 @@
             src_ref=cout.at[layer], dst_ref=cin.at[layer], send_sem=cs.at[layer],
             recv_sem=cr.at[layer], device_id={"frames": lax.rem(me + team, n)}, device_id_type=MESH,
         )
+
+    def each_mate(fn):
+        def step(k, c):
+            fn(lax.rem(lid + k, team))
+            return c
+
+        lax.fori_loop(1, team, step, 0)
 
     def unless_me(k, fn):
         @pl.when(lid != k)
@@ -235,7 +242,7 @@
                     decay = row * decay
             s1[layer, p, 0:STATE, :] = state.astype(BF16)
             s1[layer, p, STATE:, :] = decay.astype(BF16)
-            unless_me(p, lambda: gather_copy(layer, p, lid).start())
+        each_mate(lambda to: gather_copy(layer, to, lid).start())
         r1[layer, lid] = s1[layer, lid]
 
         lower = iota((SPAN, SPAN), 0) >= iota((SPAN, SPAN), 1)
@@ -283,16 +290,21 @@
 
         for k in range(team):
             s2[layer, k] = before.astype(BF16)
-            unless_me(k, lambda: return_copy(layer, k, lid).start())
             before = r1[layer, k, STATE : STATE + 1, :].astype(F32) * before + r1[
                 layer, k, 0:STATE, :
             ].astype(F32)
+        each_mate(lambda to: return_copy(layer, to, lid).start())
         r2[layer, lid] = s2[layer, lid]
         skip_row = widen(repeat_heads(jnp.broadcast_to(skip_ref[pl.ds(layer, 1), :], (16, HEADS))))
         for p in range(PAIRS):
             cols = slice(p * LANES, (p + 1) * LANES)
             skip = mm(skip_row, expand[:, cols])[0:1, :]
-            yloc[:, cols] = yloc[:, cols] + skip * act[:, cols].astype(F32)
+            for c in range(spans):
+                span = slice(c * SPAN, (c + 1) * SPAN)
+                yloc[span, cols] = yloc[span, cols] + skip * act[span, cols].astype(F32)
+                z = gate[span, cols].astype(F32)
+                swish[span, cols] = z * sigmoid(z)
+                growx[span, cols] = mm(grow[c], expand[:, cols])
 
         gain = gain_ref[pl.ds(layer, 1), :]
         for p in range(PAIRS):
@@ -301,17 +313,16 @@
             incoming = r2[layer, p]
             for c in range(spans):
                 span = slice(c * SPAN, (c + 1) * SPAN)
-                carried = mm(out_map[c], incoming) * mm(grow[c], expand[:, cols])
+                carried = mm(out_map[c], incoming) * growx[span, cols]
                 y = yloc[span, cols] + carried
-                z = gate[span, cols].astype(F32)
-                g = y * (z * sigmoid(z))
+                g = y * swish[span, cols]
                 sq = g * g
                 hi = sq.astype(BF16)
                 lo = (sq - hi.astype(F32)).astype(BF16)
                 ms = (mm(hi, ones[...]) + mm(lo, ones[...])) * (1.0 / HEAD_DIM)
                 gbuf[span, cols] = (g * lax.rsqrt(ms + HEAD_EPS) * gain[:, cols]).astype(BF16)
         weight_copy(layer, 1).wait()
-        for r in range(spans):
+        for r in reversed(range(spans)):
             span = slice(r * SPAN, (r + 1) * SPAN)
             for c in range(0, width, 256):
                 hid[span, c : c + 256] = out_ref[span, c : c + 256] + mm(
@@ -354,15 +365,13 @@
                 mstat[span, cols] = top
                 lstat[span, cols] = total
                 oacc[span, cols] = mixed
-        for c in range(spans):
+        for c in reversed(range(spans)):
+            span = slice(c * SPAN, (c + 1) * SPAN)
             rows_copy(layer, c).wait_recv()
-        a = arecv[layer]
-        for c in range(0, 2 * ATTN, 256):
-            kvp[:, c : c + 256] = mm(a, wm[layer, :, c : c + 256]).astype(BF16)
-        for p in range(ATTN // LANES):
-            cols = slice(p * LANES, (p + 1) * LANES)
-            for c in range(spans):
-                span = slice(c * SPAN, (c + 1) * SPAN)
+            for k in range(0, 2 * ATTN, 256):
+                kvp[span, k : k + 256] = mm(arecv[layer, span, :], wm[layer, :, k : k + 256]).astype(BF16)
+            for p in range(ATTN // LANES):
+                cols = slice(p * LANES, (p + 1) * LANES)
                 top, total, mixed = attend(p, span, kvp, c * SPAN, rows, rows)
                 top0 = mstat[span, cols]
                 most = jnp.maximum(top, top0)
@@ -446,6 +455,8 @@
             pltpu.VMEM((rows, ATTN), F32),
             pltpu.VMEM((rows, ATTN), F32),
             pltpu.VMEM((rows, ATTN), F32),
+            pltpu.VMEM((rows, INNER), F32),
+            pltpu.VMEM((rows, INNER), F32),
         ],
         compiler_params=pltpu.CompilerParams(
             collective_id=0, has_side_effects=True, vmem_limit_bytes=56 * 1024 * 1024

time: 68.2 us -> 65.3 us (0.957)
  Pallas kernels: 66.2 us -> 63.2 us
    pallas_call x1, Pallas kernels: 66.2 us -> 63.2 us  [shards(): pl.pallas_call(functools.partial(kernel, n), out_shape=jax.ShapeDtypeStru...]
where the time goes in v3:
time: 65.3 us; the launch traced here: 65.1 us
  Pallas kernels  63.2 us (97%)
  local copies, waits for them, and re-layouts  1.87 us (3%)
    pallas_call x1, Pallas kernels, shards(): pl.pallas_call(functools.partial(kernel, n), out_shape=jax.ShapeDtypeStru...  63.2 us
    unnamed x1, local copies, waits for them, and re-layouts  1.87 us

profile of v3, /device:TPU:0, one launch (start us, length us, event | category | flops | bytes accessed | tf_op | source)
XLA Modules:
  0.0 65.1 jit_solution(13615103709434475595)
XLA Ops:
  0.0 63.2 %shard_map.145 = f32[256,512]{1,0:T(8,128)} custom-call(bf16[256,512]{1,0:T(8,128)(2,1)} %bitcast.5, s32[8]{0:T(128)} %ts_ref.1, s32[8]{0:T(128)} %lb_ref.1, bf16[2,50,4,512]{3,2,1,0:T(4,128)(2,1)} %mod_ref.1, bf16[2,512,2304]{2,1,0:T(8,128)(2,1)} %win_hbm.1, bf16[2,16,512]{2,1,0:T(8,128)(2,1)} %bitcast.6, f32[2,4,1280]{2,1,0:T(4,128)} %conv_ref.1, ...), custom_call_target="tpu_custom_call" | custom-call | tf_op jit(solution)/shard_map/pallas_call | solution.py:413
  63.2 1.9 %copy.17 = f32[8,32,512]{2,1,0:T(8,128)} copy(f32[8,32,512]{2,1,0:T(8,128)} %bitcast.4) | data formatting | bytes 1048576

commit v4 on v3

--- a/solution.py
+++ b/solution.py
@@ -156,7 +156,7 @@
 
     def each_mate(fn):
         def step(k, c):
-            fn(lax.rem(lid + k, team))
+            fn(lax.rem(lid + lax.rem(k + team // 2 - 2, team - 1) + 1, team))
             return c
 
         lax.fori_loop(1, team, step, 0)
@@ -237,7 +237,7 @@
                 if state is None:
                     state, decay = term, row
                 else:
-                    yloc[c * SPAN : (c + 1) * SPAN, cols] = mm(out_map[c], state.astype(BF16))
+                    gbuf[(c - 1) * SPAN : c * SPAN, cols] = state.astype(BF16)
                     state = row[0:1, :] * state + term
                     decay = row * decay
             s1[layer, p, 0:STATE, :] = state.astype(BF16)
@@ -266,7 +266,8 @@
                     outs.append(mm(mixing, values))
                 y = jnp.where(first, outs[0], outs[1])
                 if c > 0:
-                    y = y + yloc[span, cols] * mm(inner_grow, expand[:, cols])
+                    inner = mm(out_map[c], gbuf[(c - 1) * SPAN : c * SPAN, cols])
+                    y = y + inner * mm(inner_grow, expand[:, cols])
                 yloc[span, cols] = y
 
         run = jnp.zeros((STATE, LANES), F32)

time: 65.3 us -> 66.6 us (1.020)
  Pallas kernels: 63.2 us -> 64.6 us
    pallas_call x1, Pallas kernels: 63.2 us -> 64.6 us  [shards(): pl.pallas_call(functools.partial(kernel, n), out_shape=jax.ShapeDtypeStru...]
where the time goes in v4:
time: 66.6 us; the launch traced here: 66.4 us
  Pallas kernels  64.6 us (97%)
  local copies, waits for them, and re-layouts  1.87 us (3%)
    pallas_call x1, Pallas kernels, shards(): pl.pallas_call(functools.partial(kernel, n), out_shape=jax.ShapeDtypeStru...  64.6 us
    unnamed x1, local copies, waits for them, and re-layouts  1.87 us

profile of v4, /device:TPU:0, one launch (start us, length us, event | category | flops | bytes accessed | tf_op | source)
XLA Modules:
  0.0 66.4 jit_solution(7817576056475778048)
XLA Ops:
  0.0 64.6 %shard_map.145 = f32[256,512]{1,0:T(8,128)} custom-call(bf16[256,512]{1,0:T(8,128)(2,1)} %bitcast.5, s32[8]{0:T(128)} %ts_ref.1, s32[8]{0:T(128)} %lb_ref.1, bf16[2,50,4,512]{3,2,1,0:T(4,128)(2,1)} %mod_ref.1, bf16[2,512,2304]{2,1,0:T(8,128)(2,1)} %win_hbm.1, bf16[2,16,512]{2,1,0:T(8,128)(2,1)} %bitcast.6, f32[2,4,1280]{2,1,0:T(4,128)} %conv_ref.1, ...), custom_call_target="tpu_custom_call" | custom-call | tf_op jit(solution)/shard_map/pallas_call | solution.py:414
  64.6 1.9 %copy.17 = f32[8,32,512]{2,1,0:T(8,128)} copy(f32[8,32,512]{2,1,0:T(8,128)} %bitcast.4) | data formatting | bytes 1048576
